TPU v7x, 128 devices: a whole 4x4x4 slice. The times are simulated.
128 devices in a mesh: cells: 128 (over z, x, y, core).
Axes of the slice: x: 4, y: 4, z: 4, core: 2. Of those that a mesh axis runs over, the one named last changes fastest.
Arguments:
- channels: float32 [256, 41, 64, 128], P('cells'), may hold values from -0.44194174 to 0.44194174, as said below
- precoders_init: float32 [256, 16, 128], P('cells'), may hold values from -1 to 1
- receiver_cells: int32 [256], replicated, may hold values from 0 to 255, as said below
- transmitter_cells: int32 [256], replicated, may hold values from 0 to 255, as said below
- interferers: int32 [256, 40], replicated, may hold values from 0 to 255, as said below
- counts: int32 [256], replicated, may hold values from 24 to 40
Outputs:
- precoders: float32 [256, 16, 128], P('cells')
- mse_weights: float32 [256, 256], P('cells')
Inputs may be any that keep to these rules, and one draw needn't show every extreme that they name: `receiver_cells`: A permutation of the cells; receiver slots s lie on device s // 2. `transmitter_cells`: A permutation of the cells; transmitter slots t lie on device t // 2. `interferers`: each row holds distinct cells, never the cell of its own receiver slot. Over the receiver slots of one device, the links in use (own links included) whose transmitter slot lies on any one device number at most 1, and 1 is reached in every draw. `channels`: own links (m = 0) are drawn stronger than interfering ones.
All inputs are finite; a program needn't handle non-finite values.
Results may differ from a plain program's by a relative error of at most 0.0003.
Values sent between devices are 32-bit elements; how exact they have to be, the bound alone decides.
A program may use at most 64 MiB of HBM per device.

v0:
```python
import jax
import jax.numpy as jnp
from jax import lax
from jax.sharding import PartitionSpec as P

LAYERS = 4
NOISE_POWER = 1.0
STEP_SIZES = (0.3, 0.2, 0.15, 0.1)
HIGHEST = lax.Precision.HIGHEST


def spd_solve(matrix, right_side):
    factor = jnp.linalg.cholesky(matrix)
    middle = lax.linalg.triangular_solve(factor, right_side, left_side=True, lower=True)
    return lax.linalg.triangular_solve(factor, middle, left_side=True, lower=True, transpose_a=True)


def link_tables(receiver_cells, transmitter_cells, interferers, counts):
    inverse = jnp.argsort(transmitter_cells)
    linked = jnp.concatenate([receiver_cells[:, None], interferers], axis=1)
    positions = inverse[linked]
    in_use = jnp.arange(interferers.shape[1] + 1, dtype=jnp.int32)[None, :] <= counts[:, None]
    return (positions, in_use)


def receiver_step(channels, link_precoders, in_use):
    weight_mask = in_use.astype(jnp.float32)
    images = jnp.einsum("klrn,kldn->kldr", channels, link_precoders, precision=HIGHEST)
    masked = images * weight_mask[:, :, None, None]
    receive_size = channels.shape[2]
    stream_count = link_precoders.shape[2]
    covariance = jnp.einsum(
        "kldr,klds->krs", masked, images, precision=HIGHEST
    ) + NOISE_POWER * jnp.eye(receive_size, dtype=jnp.float32)
    direct = images[:, 0]
    filters = spd_solve(covariance, jnp.swapaxes(direct, 1, 2))
    identity = jnp.eye(stream_count, dtype=jnp.float32)
    errors = identity - jnp.einsum("krd,ker->kde", filters, direct, precision=HIGHEST)
    weights = spd_solve(errors, jnp.broadcast_to(identity, errors.shape))
    transposed = (
        jnp.einsum("krd,klrn->kldn", filters, channels, precision=HIGHEST)
        * weight_mask[:, :, None, None]
    )
    return (weights, transposed)


def body(channels, precoders_init, receiver_cells, transmitter_cells, interferers, counts):
    devices = lax.axis_size("cells")
    own_index = lax.axis_index("cells")
    groups = channels.shape[0]
    link_count = channels.shape[1]
    streams = precoders_init.shape[1]
    antennas = precoders_init.shape[2]
    per_device = groups * link_count
    capacity = (per_device + devices - 1) // devices
    slot_total = devices * capacity
    positions, in_use = link_tables(receiver_cells, transmitter_cells, interferers, counts)
    device_of = (positions // groups).reshape(devices, per_device)
    local_of = (positions % groups).reshape(devices, per_device)
    in_service = in_use.reshape(devices, per_device)
    position_index = jnp.arange(per_device, dtype=jnp.int32)
    arriving = in_service & (device_of == own_index)
    ranked = jnp.cumsum(arriving.astype(jnp.int32), axis=1) - 1
    picker = arriving[:, None, :] & (
        ranked[:, None, :] == jnp.arange(capacity, dtype=jnp.int32)[None, :, None]
    )
    slot_used = jnp.any(picker, axis=2).reshape(-1)
    slot_local = jnp.sum(picker * local_of[:, None, :], axis=2).reshape(-1)
    slot_direct = jnp.any(
        picker & (position_index % link_count == 0)[None, None, :], axis=2
    ).reshape(-1)
    mine_device = device_of[own_index]
    mine_service = in_service[own_index]
    mine_positions = positions.reshape(devices, per_device)[own_index]
    earlier = (
        mine_service[None, :]
        & (mine_device[None, :] == mine_device[:, None])
        & (position_index[None, :] < position_index[:, None])
    )
    mine_rank = jnp.sum(earlier.astype(jnp.int32), axis=1)
    mine_index = jnp.where(mine_service, mine_device * capacity + mine_rank, 0)
    back_pick = mine_service[None, :] & (
        mine_index[None, :] == jnp.arange(slot_total, dtype=jnp.int32)[:, None]
    )
    back_used = jnp.any(back_pick, axis=1).astype(jnp.float32)
    back_position = jnp.sum(back_pick * position_index[None, :], axis=1)
    my_in_use = in_use.reshape(devices, groups, link_count)[own_index]
    target_mask = (
        (slot_local[None, :] == jnp.arange(groups, dtype=jnp.int32)[:, None]) & slot_used[None, :]
    ).astype(jnp.float32)
    direct_mask = target_mask * slot_direct.astype(jnp.float32)[None, :]
    precoders = precoders_init
    weights = jnp.zeros((groups, streams, streams), jnp.float32)
    for layer_index in range(LAYERS):
        everything = lax.all_gather(precoders, "cells", axis=0, tiled=True)
        link_precoders = everything[mine_positions]
        weights, transposed = receiver_step(
            channels, link_precoders.reshape(groups, link_count, streams, antennas), my_in_use
        )
        flat_filters = transposed.reshape(per_device, streams, antennas)
        outgoing_filters = (flat_filters[back_position] * back_used[:, None, None]).reshape(
            devices, capacity, streams, antennas
        )
        link_weights = (
            weights.reshape(groups, streams * streams)[back_position // link_count]
            * back_used[:, None]
        )
        arrived, arrived_weights = (
            lax.all_to_all(outgoing_filters, "cells", split_axis=0, concat_axis=0, tiled=True),
            lax.all_to_all(
                link_weights.reshape(devices, capacity, streams * streams),
                "cells",
                split_axis=0,
                concat_axis=0,
                tiled=True,
            ),
        )
        arrived_weights = arrived_weights.reshape(slot_total, streams, streams)
        arrived = arrived.reshape(slot_total, streams, antennas)
        weighted = jnp.einsum("sed,sen->sdn", arrived_weights, arrived, precision=HIGHEST)
        selected = target_mask[:, :, None, None] * arrived[None]
        system = jnp.einsum("gsdn,sdm->gnm", selected, weighted, precision=HIGHEST)
        system = system + STEP_SIZES[layer_index] * jnp.eye(antennas, dtype=jnp.float32)
        right_side = jnp.einsum("gs,sdn->gdn", direct_mask, weighted, precision=HIGHEST)
        precoders = jnp.swapaxes(spd_solve(system, jnp.swapaxes(right_side, 1, 2)), 1, 2)
    return (precoders, weights.reshape(groups, streams * streams))


def solution(mesh):
    return jax.shard_map(
        body,
        mesh=mesh,
        in_specs=(P("cells", None, None, None), P("cells", None, None), P(), P(), P(), P()),
        out_specs=(P("cells", None, None), P("cells", None)),
        check_vma=False,
    )
```

profile of v0, /device:TPU:1, one launch (start us, length us, event | category | flops | bytes accessed | tf_op | source)
XLA Modules:
  0.0 852.8 jit_solution(2282363171503754856)
XLA Ops:
  13.8 61.3 %gather_fusion = s32[10496]{0:T(1024)S(1)} fusion(s32[256]{0:T(256)S(1)} %get-tuple-element.6, s32[11264]{0:T(1024)S(1)} %pad_clamp_fusion), kind=kCustom, calls=%fused_computation | custom fusion | bytes 125952 | tf_op jit(solution)/shard_map/gather | solution.py:21
  83.4 5.4 broadcast_multiply_fusion.3
  92.7 12.5 %custom-call.54 = f32[2,64,64]{2,1,0:T(8,128)S(1)} custom-call(f32[2,64,64]{2,1,0:T(8,128)} %fusion.99), custom_call_target="Cholesky" | custom-call | tf_op jit(solution)/shard_map/jit(cholesky)/cholesky | solution.py:13
  106.0 10.6 %custom-call.56 = f32[2,1,64,64]{2,3,1,0:T(8,128)S(1)} custom-call(f32[2,1,64,64]{3,2,1,0:T(8,128)} %select_bitcast_fusion.7), custom_call_target="InvertDiagBlocksLowerTriangular" | custom-call | tf_op jit(solution)/shard_map/triangular_solve/custom-call.4 | solution.py:15
  130.1 12.0 %all-to-all-start.1 = ((f32[128,1,256]{2,1,0:T(1,128)}), f32[128,1,256]{2,1,0:T(1,128)}, u32[]{:S(2)}, u32[]{:S(2)}) async-start(f32[128,1,256]{2,1,0:T(1,128)} %copy.284), calls=%async_computation.1 | async-start | bytes 262144 | tf_op jit(solution)/shard_map/all_to_all | solution.py:110
  160.2 15.4 %all-to-all-done = f32[128,1,16,128]{3,2,1,0:T(8,128)} async-done(((f32[128,1,16,128]{3,2,1,0:T(8,128)}), f32[128,1,16,128]{3,2,1,0:T(8,128)}, u32[]{:S(2)}, u32[]{:S(2)}) %all-to-all-start) | async-done | bytes 1048608 | tf_op jit(solution)/shard_map/all_to_all | solution.py:109
  184.3 23.5 %custom-call.60 = f32[2,128,128]{2,1,0:T(8,128)S(1)} custom-call(f32[2,128,128]{2,1,0:T(8,128)S(1)} %fusion.79), custom_call_target="Cholesky" | custom-call | tf_op jit(solution)/shard_map/jit(cholesky)/cholesky | solution.py:13
  208.0 19.7 %custom-call.62 = f32[2,1,128,128]{2,3,1,0:T(8,128)S(1)} custom-call(f32[2,1,128,128]{3,2,1,0:T(8,128)S(1)} %select_bitcast_fusion.3), custom_call_target="InvertDiagBlocksLowerTriangular" | custom-call | tf_op jit(solution)/shard_map/triangular_solve/custom-call.8 | solution.py:15
  230.9 62.4 %all-gather.7.cloned.1.call-done = f32[256,16,128]{2,1,0:T(8,128)} async-done(((f32[2,16,128]{2,1,0:T(8,128)}), f32[256,16,128]{2,1,0:T(8,128)}) %all-gather.7.cloned.1.call-update) | async-done | bytes 2097168 | tf_op jit(solution)/shard_map/all_gather | solution.py:95
  296.5 5.4 broadcast_multiply_fusion.2
  305.9 12.6 %custom-call.63 = f32[2,64,64]{2,1,0:T(8,128)S(1)} custom-call(f32[2,64,64]{2,1,0:T(8,128)} %fusion.94), custom_call_target="Cholesky" | custom-call | tf_op jit(solution)/shard_map/jit(cholesky)/cholesky | solution.py:13
  319.3 10.6 %custom-call.65 = f32[2,1,64,64]{2,3,1,0:T(8,128)S(1)} custom-call(f32[2,1,64,64]{3,2,1,0:T(8,128)} %select_bitcast_fusion.6), custom_call_target="InvertDiagBlocksLowerTriangular" | custom-call | tf_op jit(solution)/shard_map/triangular_solve/custom-call.4 | solution.py:15
  342.7 5.8 all-to-all-start.3
  352.8 5.5 all-to-all-done.3
  366.1 16.0 %all-to-all-done.2 = f32[128,1,16,128]{3,2,1,0:T(8,128)} async-done(((f32[128,1,16,128]{3,2,1,0:T(8,128)}), f32[128,1,16,128]{3,2,1,0:T(8,128)}, u32[]{:S(2)}, u32[]{:S(2)}) %all-to-all-start.2) | async-done | bytes 1048608 | tf_op jit(solution)/shard_map/all_to_all | solution.py:109
  393.0 23.7 %custom-call.69 = f32[2,128,128]{2,1,0:T(8,128)S(1)} custom-call(f32[2,128,128]{2,1,0:T(8,128)S(1)} %fusion.75), custom_call_target="Cholesky" | custom-call | tf_op jit(solution)/shard_map/jit(cholesky)/cholesky | solution.py:13
  416.9 19.7 %custom-call.71 = f32[2,1,128,128]{2,3,1,0:T(8,128)S(1)} custom-call(f32[2,1,128,128]{3,2,1,0:T(8,128)S(1)} %select_bitcast_fusion.2), custom_call_target="InvertDiagBlocksLowerTriangular" | custom-call | tf_op jit(solution)/shard_map/triangular_solve/custom-call.8 | solution.py:15
  437.8 62.4 %all-gather.9.cloned.1.call-done = f32[256,16,128]{2,1,0:T(8,128)} async-done(((f32[2,16,128]{2,1,0:T(8,128)}), f32[256,16,128]{2,1,0:T(8,128)}) %all-gather.9.cloned.1.call-update) | async-done | bytes 2097168 | tf_op jit(solution)/shard_map/all_gather | solution.py:95
  512.7 12.9 %custom-call.72 = f32[2,64,64]{2,1,0:T(8,128)S(1)} custom-call(f32[2,64,64]{2,1,0:T(8,128)} %fusion.89), custom_call_target="Cholesky" | custom-call | tf_op jit(solution)/shard_map/jit(cholesky)/cholesky | solution.py:13
  526.4 10.6 %custom-call.74 = f32[2,1,64,64]{2,3,1,0:T(8,128)S(1)} custom-call(f32[2,1,64,64]{3,2,1,0:T(8,128)} %select_bitcast_fusion.5), custom_call_target="InvertDiagBlocksLowerTriangular" | custom-call | tf_op jit(solution)/shard_map/triangular_solve/custom-call.4 | solution.py:15
  548.5 5.8 all-to-all-start.5
  558.5 5.5 all-to-all-done.5
  571.8 16.0 %all-to-all-done.4 = f32[128,1,16,128]{3,2,1,0:T(8,128)} async-done(((f32[128,1,16,128]{3,2,1,0:T(8,128)}), f32[128,1,16,128]{3,2,1,0:T(8,128)}, u32[]{:S(2)}, u32[]{:S(2)}) %all-to-all-start.4) | async-done | bytes 1048608 | tf_op jit(solution)/shard_map/all_to_all | solution.py:109
  598.7 23.6 %custom-call.78 = f32[2,128,128]{2,1,0:T(8,128)S(1)} custom-call(f32[2,128,128]{2,1,0:T(8,128)S(1)} %fusion.71), custom_call_target="Cholesky" | custom-call | tf_op jit(solution)/shard_map/jit(cholesky)/cholesky | solution.py:13
  622.6 19.7 %custom-call.80 = f32[2,1,128,128]{2,3,1,0:T(8,128)S(1)} custom-call(f32[2,1,128,128]{3,2,1,0:T(8,128)S(1)} %select_bitcast_fusion.1), custom_call_target="InvertDiagBlocksLowerTriangular" | custom-call | tf_op jit(solution)/shard_map/triangular_solve/custom-call.8 | solution.py:15
  643.5 62.4 %all-gather.11.cloned.1.call-done = f32[256,16,128]{2,1,0:T(8,128)} async-done(((f32[2,16,128]{2,1,0:T(8,128)}), f32[256,16,128]{2,1,0:T(8,128)}) %all-gather.11.cloned.1.call-update) | async-done | bytes 2097168 | tf_op jit(solution)/shard_map/all_gather | solution.py:95
  716.9 12.5 %custom-call.81 = f32[2,64,64]{2,1,0:T(8,128)S(1)} custom-call(f32[2,64,64]{2,1,0:T(8,128)} %fusion.84), custom_call_target="Cholesky" | custom-call | tf_op jit(solution)/shard_map/jit(cholesky)/cholesky | solution.py:13
  730.3 9.8 %custom-call.83 = f32[2,1,64,64]{2,3,1,0:T(8,128)S(1)} custom-call(f32[2,1,64,64]{3,2,1,0:T(8,128)S(1)} %select_bitcast_fusion.4), custom_call_target="InvertDiagBlocksLowerTriangular" | custom-call | tf_op jit(solution)/shard_map/triangular_solve/custom-call.4 | solution.py:15
  761.0 5.6 all-to-all-done.7
  773.6 16.9 %all-to-all-done.6 = f32[128,1,16,128]{3,2,1,0:T(8,128)} async-done(((f32[128,1,16,128]{3,2,1,0:T(8,128)}), f32[128,1,16,128]{3,2,1,0:T(8,128)}, u32[]{:S(2)}, u32[]{:S(2)}) %all-to-all-start.6) | async-done | bytes 1048608 | tf_op jit(solution)/shard_map/all_to_all | solution.py:109
  801.3 23.5 %custom-call.87 = f32[2,128,128]{2,1,0:T(8,128)S(1)} custom-call(f32[2,128,128]{2,1,0:T(8,128)S(1)} %fusion.67), custom_call_target="Cholesky" | custom-call | tf_op jit(solution)/shard_map/jit(cholesky)/cholesky | solution.py:13
  825.0 19.7 %custom-call.89 = f32[2,1,128,128]{2,3,1,0:T(8,128)S(1)} custom-call(f32[2,1,128,128]{3,2,1,0:T(8,128)S(1)} %select_bitcast_fusion), custom_call_target="InvertDiagBlocksLowerTriangular" | custom-call | tf_op jit(solution)/shard_map/triangular_solve/custom-call.8 | solution.py:15
  (298 shorter events, 208.9 us)
Async XLA Ops:
  7.2 76.2 %copy-start = (f32[2,41,64,128]{3,2,1,0:T(8,128)S(1)}, f32[2,41,64,128]{3,2,1,0:T(8,128)}, u32[]{:S(2)}) copy-start(f32[2,41,64,128]{3,2,1,0:T(8,128)} %param.21) | copy-start | bytes 8060932
  7.2 73.1 %all-gather.5.cloned.1.call-start = ((), (), s32[]{:S(2)}) async-start(), calls=%async_computation.8 | async-start | bytes 2113536 | tf_op jit(solution)/shard_map/all_gather | solution.py:95
  78.9 26.2 %copy-start.10 = (pred[64,64]{1,0:T(8,128)(4,1)}, pred[64,64]{1,0:T(8,128)(4,1)S(1)}, u32[]{:S(2)}) copy-start(pred[64,64]{1,0:T(8,128)(4,1)S(1)} %iota_compare_fusion.6) | copy-start | bytes 12292
  79.8 37.2 %copy-start.13 = (f32[2,41]{1,0:T(2,128)}, f32[2,41]{1,0:T(2,128)S(1)}, u32[]{:S(2)}) copy-start(f32[2,41]{1,0:T(2,128)S(1)} %fusion.166) | copy-start | bytes 988
  88.7 28.0 %copy-start.7 = (f32[2,41,16,64]{3,2,1,0:T(8,128)}, f32[2,41,16,64]{3,2,1,0:T(8,128)S(1)}, u32[]{:S(2)}) copy-start(f32[2,41,16,64]{3,2,1,0:T(8,128)S(1)} %get-tuple-element.24) | copy-start | bytes 1007620
  130.1 21.8 %all-to-all-start.1 = ((f32[128,1,256]{2,1,0:T(1,128)}), f32[128,1,256]{2,1,0:T(1,128)}, u32[]{:S(2)}, u32[]{:S(2)}) async-start(f32[128,1,256]{2,1,0:T(1,128)} %copy.284), calls=%async_computation.1 | async-start | bytes 262144 | tf_op jit(solution)/shard_map/all_to_all | solution.py:110
  151.9 23.8 %all-to-all-start = ((f32[128,1,16,128]{3,2,1,0:T(8,128)}), f32[128,1,16,128]{3,2,1,0:T(8,128)}, u32[]{:S(2)}, u32[]{:S(2)}) async-start(f32[128,1,16,128]{3,2,1,0:T(8,128)} %bitcast_multiply_fusion.3), calls=%async_computation | async-start | bytes 2097152 | tf_op jit(solution)/shard_map/all_to_all | solution.py:109
  157.1 136.3 %all-gather.7.cloned.1.call-start = ((), (), s32[]{:S(2)}) async-start(), calls=%async_computation.9 | async-start | bytes 2113536 | tf_op jit(solution)/shard_map/all_gather | solution.py:95
  157.7 69.9 %copy-start.31 = (f32[128]{0:T(128)}, f32[128]{0:T(128)S(1)}, u32[]{:S(2)}) copy-start(f32[128]{0:T(128)S(1)} %convert_element_type.98) | copy-start | bytes 1540
  157.8 23.2 %copy-start.22 = (f32[2,128]{1,0:T(2,128)}, f32[2,128]{1,0:T(2,128)S(1)}, u32[]{:S(2)}) copy-start(f32[2,128]{1,0:T(2,128)S(1)} %get-tuple-element.12) | copy-start | bytes 3076
  157.8 69.8 %copy-start.26 = (pred[2,128]{1,0:T(4,128)(4,1)}, pred[2,128]{1,0:T(4,128)(4,1)S(1)}, u32[]{:S(2)}) copy-start(pred[2,128]{1,0:T(4,128)(4,1)S(1)} %get-tuple-element.14) | copy-start | bytes 772
  182.0 114.5 %copy-start.14 = (f32[2,41]{1,0:T(2,128)S(1)}, f32[2,41]{1,0:T(2,128)}, u32[]{:S(2)}) copy-start(f32[2,41]{1,0:T(2,128)} %copy-done.13) | copy-start | bytes 988
  342.7 15.6 %all-to-all-start.3 = ((f32[128,1,256]{2,1,0:T(1,128)}), f32[128,1,256]{2,1,0:T(1,128)}, u32[]{:S(2)}, u32[]{:S(2)}) async-start(f32[128,1,256]{2,1,0:T(1,128)} %copy.308), calls=%async_computation.3 | async-start | bytes 262144 | tf_op jit(solution)/shard_map/all_to_all | solution.py:110
  358.3 23.8 %all-to-all-start.2 = ((f32[128,1,16,128]{3,2,1,0:T(8,128)}), f32[128,1,16,128]{3,2,1,0:T(8,128)}, u32[]{:S(2)}, u32[]{:S(2)}) async-start(f32[128,1,16,128]{3,2,1,0:T(8,128)} %bitcast_multiply_fusion.2), calls=%async_computation.2 | async-start | bytes 2097152 | tf_op jit(solution)/shard_map/all_to_all | solution.py:109
  363.5 22.3 %copy-start.27 = (pred[2,128]{1,0:T(4,128)(4,1)S(1)}, pred[2,128]{1,0:T(4,128)(4,1)}, u32[]{:S(2)}) copy-start(pred[2,128]{1,0:T(4,128)(4,1)} %copy-done.26) | copy-start | bytes 772
  363.5 22.2 %copy-start.32 = (f32[128]{0:T(128)S(1)}, f32[128]{0:T(128)}, u32[]{:S(2)}) copy-start(f32[128]{0:T(128)} %copy-done.31) | copy-start | bytes 1540
  363.5 136.6 %all-gather.9.cloned.1.call-start = ((), (), s32[]{:S(2)}) async-start(), calls=%async_computation.10 | async-start | bytes 2113536 | tf_op jit(solution)/shard_map/all_gather | solution.py:95
  366.0 23.2 %copy-start.23 = (f32[2,128]{1,0:T(2,128)S(1)}, f32[2,128]{1,0:T(2,128)}, u32[]{:S(2)}) copy-start(f32[2,128]{1,0:T(2,128)} %copy-done.22) | copy-start | bytes 3076
  508.7 33.3 %copy-start.17 = (pred[16,16]{1,0:T(8,128)(4,1)S(1)}, pred[16,16]{1,0:T(8,128)(4,1)}, u32[]{:S(2)}) copy-start(pred[16,16]{1,0:T(8,128)(4,1)} %iota_compare_fusion.9) | copy-start | bytes 772
  508.7 33.4 %copy-start.15 = (pred[16,16]{1,0:T(8,128)(4,1)S(1)}, pred[16,16]{1,0:T(8,128)(4,1)}, u32[]{:S(2)}) copy-start(pred[16,16]{1,0:T(8,128)(4,1)} %iota_compare_fusion.8) | copy-start | bytes 772
  548.5 15.6 %all-to-all-start.5 = ((f32[128,1,256]{2,1,0:T(1,128)}), f32[128,1,256]{2,1,0:T(1,128)}, u32[]{:S(2)}, u32[]{:S(2)}) async-start(f32[128,1,256]{2,1,0:T(1,128)} %copy.332), calls=%async_computation.5 | async-start | bytes 262144 | tf_op jit(solution)/shard_map/all_to_all | solution.py:110
  564.1 23.8 %all-to-all-start.4 = ((f32[128,1,16,128]{3,2,1,0:T(8,128)}), f32[128,1,16,128]{3,2,1,0:T(8,128)}, u32[]{:S(2)}, u32[]{:S(2)}) async-start(f32[128,1,16,128]{3,2,1,0:T(8,128)} %bitcast_multiply_fusion.1), calls=%async_computation.4 | async-start | bytes 2097152 | tf_op jit(solution)/shard_map/all_to_all | solution.py:109
  569.2 22.3 %copy-start.28 = (pred[2,128]{1,0:T(4,128)(4,1)S(1)}, pred[2,128]{1,0:T(4,128)(4,1)}, u32[]{:S(2)}) copy-start(pred[2,128]{1,0:T(4,128)(4,1)} %copy-done.26) | copy-start | bytes 772
  569.3 22.2 %copy-start.33 = (f32[128]{0:T(128)S(1)}, f32[128]{0:T(128)}, u32[]{:S(2)}) copy-start(f32[128]{0:T(128)} %copy-done.31) | copy-start | bytes 1540
  569.3 136.6 %all-gather.11.cloned.1.call-start = ((), (), s32[]{:S(2)}) async-start(), calls=%async_computation.11 | async-start | bytes 2113536 | tf_op jit(solution)/shard_map/all_gather | solution.py:95
  571.8 23.2 %copy-start.24 = (f32[2,128]{1,0:T(2,128)S(1)}, f32[2,128]{1,0:T(2,128)}, u32[]{:S(2)}) copy-start(f32[2,128]{1,0:T(2,128)} %copy-done.22) | copy-start | bytes 3076
  716.2 29.6 %copy-start.18 = (pred[16,16]{1,0:T(8,128)(4,1)S(1)}, pred[16,16]{1,0:T(8,128)(4,1)}, u32[]{:S(2)}) copy-start(pred[16,16]{1,0:T(8,128)(4,1)} %iota_compare_fusion.9) | copy-start | bytes 772
  716.2 29.8 %copy-start.16 = (pred[16,16]{1,0:T(8,128)(4,1)S(1)}, pred[16,16]{1,0:T(8,128)(4,1)}, u32[]{:S(2)}) copy-start(pred[16,16]{1,0:T(8,128)(4,1)} %iota_compare_fusion.8) | copy-start | bytes 772
  751.3 15.3 %all-to-all-start.7 = ((f32[128,1,256]{2,1,0:T(1,128)}), f32[128,1,256]{2,1,0:T(1,128)S(1)}, u32[]{:S(2)}, u32[]{:S(2)}) async-start(f32[128,1,256]{2,1,0:T(1,128)} %copy.356), calls=%async_computation.7 | async-start | bytes 262144 | tf_op jit(solution)/shard_map/all_to_all | solution.py:110
  766.7 23.8 %all-to-all-start.6 = ((f32[128,1,16,128]{3,2,1,0:T(8,128)}), f32[128,1,16,128]{3,2,1,0:T(8,128)}, u32[]{:S(2)}, u32[]{:S(2)}) async-start(f32[128,1,16,128]{3,2,1,0:T(8,128)} %bitcast_multiply_fusion), calls=%async_computation.6 | async-start | bytes 2097152 | tf_op jit(solution)/shard_map/all_to_all | solution.py:109
  772.0 22.1 %copy-start.29 = (pred[2,128]{1,0:T(4,128)(4,1)S(1)}, pred[2,128]{1,0:T(4,128)(4,1)}, u32[]{:S(2)}) copy-start(pred[2,128]{1,0:T(4,128)(4,1)} %copy-done.26) | copy-start | bytes 772
  773.6 24.1 %copy-start.25 = (f32[2,128]{1,0:T(2,128)S(1)}, f32[2,128]{1,0:T(2,128)}, u32[]{:S(2)}) copy-start(f32[2,128]{1,0:T(2,128)} %copy-done.22) | copy-start | bytes 3076
  (17 other events, 182.5 us)
Sparse Core Ops, SparseCore 0:
  11.1 69.1 all-gather.4
  231.1 62.2 all-gather.6
  437.9 62.2 all-gather.8
  643.6 62.2 all-gather.10
where the time goes:
time: 864 us; the launch traced here: 853 us
  other arithmetic  322 us (37%)
  waiting for transfers between devices  275 us (32%)
  local copies, waits for them, and re-layouts  119 us (14%)
  matrix products  72.2 us (8%)
  starting transfers between devices  49.9 us (6%)
  between operations  15.1 us (2%)
    all_gather x4, waiting for transfers between devices, body(): everything = lax.all_gather(precoders, 'cells', axis=0, tiled=True)  188 us
    another operation x39, other arithmetic, spd_solve(): factor = jnp.linalg.cholesky(matrix)  161 us
    another operation x27, other arithmetic, spd_solve(): lax.linalg.triangular_solve(factor, middle, left_side=True, lower=True, t...  135 us
    all_to_all x4, waiting for transfers between devices, body(): lax.all_to_all(outgoing_filters, 'cells', split_axis=0, concat_axis=0, ti...  64.3 us
    gather x5, local copies, waits for them, and re-layouts, link_tables(): positions = inverse[linked]  61.7 us
    all_to_all x4, starting transfers between devices, body(): lax.all_to_all(link_weights.reshape(devices, capacity, streams * streams)...  28.9 us
    all_to_all x4, waiting for transfers between devices, body(): lax.all_to_all(link_weights.reshape(devices, capacity, streams * streams)...  22 us
    dot_general x4, matrix products, receiver_step(): jnp.einsum('klrn,kldn->kldr', channels, link_precoders, precision=HIGHEST)  21.5 us
  transfers between devices with their start and end apart: 12, of which 12 were waited for; matrix products, arithmetic and copies ran while one was open for 12% of the time, Pallas kernels for 0%

commit v1 on v0

--- a/solution.py
+++ b/solution.py
@@ -92,7 +92,10 @@
     precoders = precoders_init
     weights = jnp.zeros((groups, streams, streams), jnp.float32)
     for layer_index in range(LAYERS):
-        everything = lax.all_gather(precoders, "cells", axis=0, tiled=True)
+        size = lax.axis_size("cells")
+        pieces = jnp.stack([precoders for _ in range(size)])
+        pieces = lax.all_to_all(pieces, "cells", split_axis=0, concat_axis=0)
+        everything = jnp.concatenate(pieces, axis=0)
         link_precoders = everything[mine_positions]
         weights, transposed = receiver_step(
             channels, link_precoders.reshape(groups, link_count, streams, antennas), my_in_use

time: 864 us -> 768 us (0.89)
  waiting for transfers between devices: 275 us -> 94.7 us
  blocking collectives: 0 us -> 106 us
  between operations: 15.1 us -> 2.11 us
    all_gather x4 -> x0, waiting for transfers between devices: 188 us -> none  [body(): everything = lax.all_gather(precoders, 'cells', axis=0, tiled=True)]
    all_to_all x0 -> x3, blocking collectives: none -> 106 us  [body(): pieces = lax.all_to_all(pieces, 'cells', split_axis=0, concat_axis=0)]
    all_to_all x0 -> x1, starting transfers between devices: none -> 12 us  [body(): pieces = lax.all_to_all(pieces, 'cells', split_axis=0, concat_axis=0)]
  transfers between devices with their start and end apart: 12 -> 9, of which waited for: 12 -> 8; matrix products, arithmetic and copies ran while one was open for 12% -> 11% of each run, Pallas kernels for 0% -> 0%
where the time goes in v1:
time: 768 us; the launch traced here: 757 us
  other arithmetic  314 us (41%)
  local copies, waits for them, and re-layouts  115 us (15%)
  blocking collectives  106 us (14%)
  waiting for transfers between devices  94.7 us (12%)
  matrix products  67.5 us (9%)
  starting transfers between devices  57.5 us (7%)
    another operation x39, other arithmetic, spd_solve(): factor = jnp.linalg.cholesky(matrix)  157 us
    another operation x27, other arithmetic, spd_solve(): lax.linalg.triangular_solve(factor, middle, left_side=True, lower=True, t...  134 us
    all_to_all x3, blocking collectives, body(): pieces = lax.all_to_all(pieces, 'cells', split_axis=0, concat_axis=0)  106 us
    all_to_all x4, waiting for transfers between devices, body(): lax.all_to_all(outgoing_filters, 'cells', split_axis=0, concat_axis=0, ti...  66 us
    gather x5, local copies, waits for them, and re-layouts, link_tables(): positions = inverse[linked]  61.7 us
    all_to_all x4, waiting for transfers between devices, body(): lax.all_to_all(link_weights.reshape(devices, capacity, streams * streams)...  28.7 us
    all_to_all x4, starting transfers between devices, body(): lax.all_to_all(link_weights.reshape(devices, capacity, streams * streams)...  24.3 us
    dot_general x4, matrix products, receiver_step(): jnp.einsum('klrn,kldn->kldr', channels, link_precoders, precision=HIGHEST)  21.5 us
  transfers between devices with their start and end apart: 9, of which 8 were waited for; matrix products, arithmetic and copies ran while one was open for 11% of the time, Pallas kernels for 0%

profile of v1, /device:TPU:1, one launch (start us, length us, event | category | flops | bytes accessed | tf_op | source)
XLA Modules:
  0.0 756.8 jit_solution(2552601756321907480)
XLA Ops:
  3.1 12.0 %all-to-all-start = ((f32[128,2,16,128]{3,2,1,0:T(8,128)}), f32[128,2,16,128]{3,2,1,0:T(8,128)}, u32[]{:S(2)}, u32[]{:S(2)}) async-start(f32[128,2,16,128]{3,2,1,0:T(8,128)} %stack.8), calls=%async_computation | async-start | bytes 4194304 | tf_op jit(solution)/shard_map/all_to_all | solution.py:97
  18.8 61.3 %gather_fusion = s32[10496]{0:T(1024)S(1)} fusion(s32[256]{0:T(256)S(1)} %get-tuple-element.6, s32[11264]{0:T(1024)S(1)} %pad_clamp_fusion), kind=kCustom, calls=%fused_computation | custom fusion | bytes 125952 | tf_op jit(solution)/shard_map/gather | solution.py:21
  85.6 5.4 broadcast_multiply_fusion.3
  94.9 12.5 %custom-call.54 = f32[2,64,64]{2,1,0:T(8,128)S(1)} custom-call(f32[2,64,64]{2,1,0:T(8,128)} %fusion.99), custom_call_target="Cholesky" | custom-call | tf_op jit(solution)/shard_map/jit(cholesky)/cholesky | solution.py:13
  108.3 10.6 %custom-call.56 = f32[2,1,64,64]{2,3,1,0:T(8,128)S(1)} custom-call(f32[2,1,64,64]{3,2,1,0:T(8,128)} %select_bitcast_fusion.7), custom_call_target="InvertDiagBlocksLowerTriangular" | custom-call | tf_op jit(solution)/shard_map/triangular_solve/custom-call.4 | solution.py:15
  130.9 10.2 %all-to-all-start.2 = ((f32[128,1,256]{2,1,0:T(1,128)}), f32[128,1,256]{2,1,0:T(1,128)}, u32[]{:S(2)}, u32[]{:S(2)}) async-start(f32[128,1,256]{2,1,0:T(1,128)} %copy.284), calls=%async_computation.2 | async-start | bytes 262144 | tf_op jit(solution)/shard_map/all_to_all | solution.py:113
  145.4 5.5 all-to-all-done.2
  159.2 15.5 %all-to-all-done.1 = f32[128,1,16,128]{3,2,1,0:T(8,128)} async-done(((f32[128,1,16,128]{3,2,1,0:T(8,128)}), f32[128,1,16,128]{3,2,1,0:T(8,128)}, u32[]{:S(2)}, u32[]{:S(2)}) %all-to-all-start.1) | async-done | bytes 1048608 | tf_op jit(solution)/shard_map/all_to_all | solution.py:112
  183.3 23.5 %custom-call.60 = f32[2,128,128]{2,1,0:T(8,128)S(1)} custom-call(f32[2,128,128]{2,1,0:T(8,128)S(1)} %fusion.79), custom_call_target="Cholesky" | custom-call | tf_op jit(solution)/shard_map/jit(cholesky)/cholesky | solution.py:13
  207.0 19.7 %custom-call.62 = f32[2,1,128,128]{2,3,1,0:T(8,128)S(1)} custom-call(f32[2,1,128,128]{3,2,1,0:T(8,128)S(1)} %select_bitcast_fusion.3), custom_call_target="InvertDiagBlocksLowerTriangular" | custom-call | tf_op jit(solution)/shard_map/triangular_solve/custom-call.8 | solution.py:15
  229.6 35.2 %all_to_all.60 = f32[128,2,16,128]{3,2,1,0:T(8,128)} all-to-all(f32[128,2,16,128]{3,2,1,0:T(8,128)S(1)} %stack.9), channel_id=1, replica_groups=mesh['cells'=128] {'cells'}, dimensions={0} | all-to-all | bytes 4194304 | tf_op jit(solution)/shard_map/all_to_all | solution.py:97
  277.3 12.5 %custom-call.63 = f32[2,64,64]{2,1,0:T(8,128)S(1)} custom-call(f32[2,64,64]{2,1,0:T(8,128)} %fusion.94), custom_call_target="Cholesky" | custom-call | tf_op jit(solution)/shard_map/jit(cholesky)/cholesky | solution.py:13
  290.6 10.6 %custom-call.65 = f32[2,1,64,64]{2,3,1,0:T(8,128)S(1)} custom-call(f32[2,1,64,64]{3,2,1,0:T(8,128)} %select_bitcast_fusion.6), custom_call_target="InvertDiagBlocksLowerTriangular" | custom-call | tf_op jit(solution)/shard_map/triangular_solve/custom-call.4 | solution.py:15
  320.8 7.7 %all-to-all-done.5 = f32[128,1,256]{2,1,0:T(1,128)S(1)} async-done(((f32[128,1,256]{2,1,0:T(1,128)}), f32[128,1,256]{2,1,0:T(1,128)S(1)}, u32[]{:S(2)}, u32[]{:S(2)}) %all-to-all-start.5) | async-done | bytes 131104 | tf_op jit(solution)/shard_map/all_to_all | solution.py:113
  335.4 16.8 %all-to-all-done.4 = f32[128,1,16,128]{3,2,1,0:T(8,128)} async-done(((f32[128,1,16,128]{3,2,1,0:T(8,128)}), f32[128,1,16,128]{3,2,1,0:T(8,128)}, u32[]{:S(2)}, u32[]{:S(2)}) %all-to-all-start.4) | async-done | bytes 1048608 | tf_op jit(solution)/shard_map/all_to_all | solution.py:112
  360.7 23.5 %custom-call.69 = f32[2,128,128]{2,1,0:T(8,128)S(1)} custom-call(f32[2,128,128]{2,1,0:T(8,128)S(1)} %fusion.75), custom_call_target="Cholesky" | custom-call | tf_op jit(solution)/shard_map/jit(cholesky)/cholesky | solution.py:13
  384.5 19.7 %custom-call.71 = f32[2,1,128,128]{2,3,1,0:T(8,128)S(1)} custom-call(f32[2,1,128,128]{3,2,1,0:T(8,128)S(1)} %select_bitcast_fusion.2), custom_call_target="InvertDiagBlocksLowerTriangular" | custom-call | tf_op jit(solution)/shard_map/triangular_solve/custom-call.8 | solution.py:15
  405.0 35.4 %all_to_all.61 = f32[128,2,16,128]{3,2,1,0:T(8,128)} all-to-all(f32[128,2,16,128]{3,2,1,0:T(8,128)S(1)} %stack.10), channel_id=1, replica_groups=mesh['cells'=128] {'cells'}, dimensions={0} | all-to-all | bytes 4194304 | tf_op jit(solution)/shard_map/all_to_all | solution.py:97
  452.9 12.5 %custom-call.72 = f32[2,64,64]{2,1,0:T(8,128)S(1)} custom-call(f32[2,64,64]{2,1,0:T(8,128)} %fusion.89), custom_call_target="Cholesky" | custom-call | tf_op jit(solution)/shard_map/jit(cholesky)/cholesky | solution.py:13
  466.2 10.6 %custom-call.74 = f32[2,1,64,64]{2,3,1,0:T(8,128)S(1)} custom-call(f32[2,1,64,64]{3,2,1,0:T(8,128)} %select_bitcast_fusion.5), custom_call_target="InvertDiagBlocksLowerTriangular" | custom-call | tf_op jit(solution)/shard_map/triangular_solve/custom-call.4 | solution.py:15
  496.4 7.7 %all-to-all-done.8 = f32[128,1,256]{2,1,0:T(1,128)S(1)} async-done(((f32[128,1,256]{2,1,0:T(1,128)}), f32[128,1,256]{2,1,0:T(1,128)S(1)}, u32[]{:S(2)}, u32[]{:S(2)}) %all-to-all-start.8) | async-done | bytes 131104 | tf_op jit(solution)/shard_map/all_to_all | solution.py:113
  511.0 16.8 %all-to-all-done.7 = f32[128,1,16,128]{3,2,1,0:T(8,128)} async-done(((f32[128,1,16,128]{3,2,1,0:T(8,128)}), f32[128,1,16,128]{3,2,1,0:T(8,128)}, u32[]{:S(2)}, u32[]{:S(2)}) %all-to-all-start.7) | async-done | bytes 1048608 | tf_op jit(solution)/shard_map/all_to_all | solution.py:112
  536.3 23.5 %custom-call.78 = f32[2,128,128]{2,1,0:T(8,128)S(1)} custom-call(f32[2,128,128]{2,1,0:T(8,128)S(1)} %fusion.71), custom_call_target="Cholesky" | custom-call | tf_op jit(solution)/shard_map/jit(cholesky)/cholesky | solution.py:13
  560.0 19.7 %custom-call.80 = f32[2,1,128,128]{2,3,1,0:T(8,128)S(1)} custom-call(f32[2,1,128,128]{3,2,1,0:T(8,128)S(1)} %select_bitcast_fusion.1), custom_call_target="InvertDiagBlocksLowerTriangular" | custom-call | tf_op jit(solution)/shard_map/triangular_solve/custom-call.8 | solution.py:15
  580.5 35.2 %all_to_all.62 = f32[128,2,16,128]{3,2,1,0:T(8,128)} all-to-all(f32[128,2,16,128]{3,2,1,0:T(8,128)S(1)} %stack.11), channel_id=1, replica_groups=mesh['cells'=128] {'cells'}, dimensions={0} | all-to-all | bytes 4194304 | tf_op jit(solution)/shard_map/all_to_all | solution.py:97
  628.2 12.5 %custom-call.81 = f32[2,64,64]{2,1,0:T(8,128)S(1)} custom-call(f32[2,64,64]{2,1,0:T(8,128)} %fusion.84), custom_call_target="Cholesky" | custom-call | tf_op jit(solution)/shard_map/jit(cholesky)/cholesky | solution.py:13
  641.6 10.6 %custom-call.83 = f32[2,1,64,64]{2,3,1,0:T(8,128)S(1)} custom-call(f32[2,1,64,64]{3,2,1,0:T(8,128)} %select_bitcast_fusion.4), custom_call_target="InvertDiagBlocksLowerTriangular" | custom-call | tf_op jit(solution)/shard_map/triangular_solve/custom-call.4 | solution.py:15
  671.8 7.7 %all-to-all-done.11 = f32[128,1,256]{2,1,0:T(1,128)S(1)} async-done(((f32[128,1,256]{2,1,0:T(1,128)}), f32[128,1,256]{2,1,0:T(1,128)S(1)}, u32[]{:S(2)}, u32[]{:S(2)}) %all-to-all-start.11) | async-done | bytes 131104 | tf_op jit(solution)/shard_map/all_to_all | solution.py:113
  679.5 5.4 all-to-all-start.10
  686.4 16.9 %all-to-all-done.10 = f32[128,1,16,128]{3,2,1,0:T(8,128)} async-done(((f32[128,1,16,128]{3,2,1,0:T(8,128)}), f32[128,1,16,128]{3,2,1,0:T(8,128)}, u32[]{:S(2)}, u32[]{:S(2)}) %all-to-all-start.10) | async-done | bytes 1048608 | tf_op jit(solution)/shard_map/all_to_all | solution.py:112
  711.8 23.5 %custom-call.87 = f32[2,128,128]{2,1,0:T(8,128)S(1)} custom-call(f32[2,128,128]{2,1,0:T(8,128)S(1)} %fusion.67), custom_call_target="Cholesky" | custom-call | tf_op jit(solution)/shard_map/jit(cholesky)/cholesky | solution.py:13
  735.6 19.7 %custom-call.89 = f32[2,1,128,128]{2,3,1,0:T(8,128)S(1)} custom-call(f32[2,1,128,128]{3,2,1,0:T(8,128)S(1)} %select_bitcast_fusion), custom_call_target="InvertDiagBlocksLowerTriangular" | custom-call | tf_op jit(solution)/shard_map/triangular_solve/custom-call.8 | solution.py:15
  (275 shorter events, 195.2 us)
Async XLA Ops:
  0.6 85.0 %copy-start = (f32[2,41,64,128]{3,2,1,0:T(8,128)S(1)}, f32[2,41,64,128]{3,2,1,0:T(8,128)}, u32[]{:S(2)}) copy-start(f32[2,41,64,128]{3,2,1,0:T(8,128)} %param.21) | copy-start | bytes 8060932
  3.1 12.0 %copy-start.24 = (s32[256]{0:T(256)S(1)}, s32[256]{0:T(256)}, u32[]{:S(2)}) copy-start(s32[256]{0:T(256)} %param.26) | copy-start | bytes 3076
  3.1 12.1 %copy-start.14 = (s32[256,40]{0,1:T(8,128)S(1)}, s32[256,40]{0,1:T(8,128)}, u32[]{:S(2)}) copy-start(s32[256,40]{0,1:T(8,128)} %param.25) | copy-start | bytes 122884
  3.1 12.1 %copy-start.25 = (s32[256]{0:T(256)S(1)}, s32[256]{0:T(256)}, u32[]{:S(2)}) copy-start(s32[256]{0:T(256)} %param.23) | copy-start | bytes 3076
  3.1 12.5 %copy-start.26 = (s32[256]{0:T(256)S(1)}, s32[256]{0:T(256)}, u32[]{:S(2)}) copy-start(s32[256]{0:T(256)} %param.24) | copy-start | bytes 3076
  3.1 79.5 %all-to-all-start = ((f32[128,2,16,128]{3,2,1,0:T(8,128)}), f32[128,2,16,128]{3,2,1,0:T(8,128)}, u32[]{:S(2)}, u32[]{:S(2)}) async-start(f32[128,2,16,128]{3,2,1,0:T(8,128)} %stack.8), calls=%async_computation | async-start | bytes 4194304 | tf_op jit(solution)/shard_map/all_to_all | solution.py:97
  80.3 5.3 copy-start.11
  80.5 5.2 copy-start.22
  82.3 8.7 %copy-start.15 = (s32[1024]{0:T(1024)}, s32[1024]{0:T(1024)S(1)}, u32[]{:S(2)}) copy-start(s32[1024]{0:T(1024)S(1)} %pad_clamp_fusion.3) | copy-start | bytes 12292
  82.5 45.2 %copy-start.16 = (s32[1024]{0:T(1024)}, s32[1024]{0:T(1024)S(1)}, u32[]{:S(2)}) copy-start(s32[1024]{0:T(1024)S(1)} %get-tuple-element.31) | copy-start | bytes 12292
  82.5 58.6 %copy-start.17 = (s32[1024]{0:T(1024)}, s32[1024]{0:T(1024)S(1)}, u32[]{:S(2)}) copy-start(s32[1024]{0:T(1024)S(1)} %get-tuple-element.32) | copy-start | bytes 12292
  91.0 28.0 %copy-start.8 = (f32[2,41,16,64]{3,2,1,0:T(8,128)}, f32[2,41,16,64]{3,2,1,0:T(8,128)S(1)}, u32[]{:S(2)}) copy-start(f32[2,41,16,64]{3,2,1,0:T(8,128)S(1)} %get-tuple-element.24) | copy-start | bytes 1007620
  130.9 20.0 %all-to-all-start.2 = ((f32[128,1,256]{2,1,0:T(1,128)}), f32[128,1,256]{2,1,0:T(1,128)}, u32[]{:S(2)}, u32[]{:S(2)}) async-start(f32[128,1,256]{2,1,0:T(1,128)} %copy.284), calls=%async_computation.2 | async-start | bytes 262144 | tf_op jit(solution)/shard_map/all_to_all | solution.py:113
  142.9 13.3 %copy-start.12 = (s32[128,2,41]{0,2,1:T(8,128)S(1)}, s32[128,2,41]{0,2,1:T(8,128)}, u32[]{:S(2)}) copy-start(s32[128,2,41]{0,2,1:T(8,128)} %copy-done.11) | copy-start | bytes 125956
  142.9 13.5 %copy-start.13 = (s32[128,82]{0,1:T(8,128)S(1)}, s32[128,82]{0,1:T(8,128)}, u32[]{:S(2)}) copy-start(s32[128,82]{0,1:T(8,128)} %get-tuple-element.19) | copy-start | bytes 125956
  142.9 13.6 %copy-start.23 = (s32[82]{0:T(128)S(1)}, s32[82]{0:T(128)}, u32[]{:S(2)}) copy-start(s32[82]{0:T(128)} %copy-done.22) | copy-start | bytes 988
  150.9 23.8 %all-to-all-start.1 = ((f32[128,1,16,128]{3,2,1,0:T(8,128)}), f32[128,1,16,128]{3,2,1,0:T(8,128)}, u32[]{:S(2)}, u32[]{:S(2)}) async-start(f32[128,1,16,128]{3,2,1,0:T(8,128)} %bitcast_multiply_fusion.3), calls=%async_computation.1 | async-start | bytes 2097152 | tf_op jit(solution)/shard_map/all_to_all | solution.py:112
  156.7 70.0 %copy-start.18 = (f32[128]{0:T(128)}, f32[128]{0:T(128)S(1)}, u32[]{:S(2)}) copy-start(f32[128]{0:T(128)S(1)} %convert_element_type.98) | copy-start | bytes 1540
  177.3 3.8 copy-start.6
  273.3 28.0 %copy-start.9 = (f32[2,41,16,64]{3,2,1,0:T(8,128)}, f32[2,41,16,64]{3,2,1,0:T(8,128)S(1)}, u32[]{:S(2)}) copy-start(f32[2,41,16,64]{3,2,1,0:T(8,128)S(1)} %get-tuple-element.26) | copy-start | bytes 1007620
  313.6 14.9 %all-to-all-start.5 = ((f32[128,1,256]{2,1,0:T(1,128)}), f32[128,1,256]{2,1,0:T(1,128)S(1)}, u32[]{:S(2)}, u32[]{:S(2)}) async-start(f32[128,1,256]{2,1,0:T(1,128)} %copy.308), calls=%async_computation.5 | async-start | bytes 262144 | tf_op jit(solution)/shard_map/all_to_all | solution.py:113
  328.5 23.8 %all-to-all-start.4 = ((f32[128,1,16,128]{3,2,1,0:T(8,128)}), f32[128,1,16,128]{3,2,1,0:T(8,128)}, u32[]{:S(2)}, u32[]{:S(2)}) async-start(f32[128,1,16,128]{3,2,1,0:T(8,128)} %bitcast_multiply_fusion.2), calls=%async_computation.4 | async-start | bytes 2097152 | tf_op jit(solution)/shard_map/all_to_all | solution.py:112
  354.9 3.7 copy-start.4
  448.9 28.0 %copy-start.10 = (f32[2,41,16,64]{3,2,1,0:T(8,128)}, f32[2,41,16,64]{3,2,1,0:T(8,128)S(1)}, u32[]{:S(2)}) copy-start(f32[2,41,16,64]{3,2,1,0:T(8,128)S(1)} %get-tuple-element.28) | copy-start | bytes 1007620
  489.2 14.9 %all-to-all-start.8 = ((f32[128,1,256]{2,1,0:T(1,128)}), f32[128,1,256]{2,1,0:T(1,128)S(1)}, u32[]{:S(2)}, u32[]{:S(2)}) async-start(f32[128,1,256]{2,1,0:T(1,128)} %copy.332), calls=%async_computation.8 | async-start | bytes 262144 | tf_op jit(solution)/shard_map/all_to_all | solution.py:113
  504.1 23.7 %all-to-all-start.7 = ((f32[128,1,16,128]{3,2,1,0:T(8,128)}), f32[128,1,16,128]{3,2,1,0:T(8,128)}, u32[]{:S(2)}, u32[]{:S(2)}) async-start(f32[128,1,16,128]{3,2,1,0:T(8,128)} %bitcast_multiply_fusion.1), calls=%async_computation.7 | async-start | bytes 2097152 | tf_op jit(solution)/shard_map/all_to_all | solution.py:112
  530.4 3.7 copy-start.5
  624.3 28.0 %copy-start.7 = (f32[2,41,16,64]{3,2,1,0:T(8,128)}, f32[2,41,16,64]{3,2,1,0:T(8,128)S(1)}, u32[]{:S(2)}) copy-start(f32[2,41,16,64]{3,2,1,0:T(8,128)S(1)} %get-tuple-element.30) | copy-start | bytes 1007620
  662.9 16.6 %copy-start.1 = (f32[2,256]{1,0:T(2,128)}, f32[2,256]{1,0:T(2,128)S(1)}, u32[]{:S(2)}) copy-start(f32[2,256]{1,0:T(2,128)S(1)} %reshape.867) | copy-start | bytes 6148
  664.7 14.9 %all-to-all-start.11 = ((f32[128,1,256]{2,1,0:T(1,128)}), f32[128,1,256]{2,1,0:T(1,128)S(1)}, u32[]{:S(2)}, u32[]{:S(2)}) async-start(f32[128,1,256]{2,1,0:T(1,128)} %copy.356), calls=%async_computation.11 | async-start | bytes 262144 | tf_op jit(solution)/shard_map/all_to_all | solution.py:113
  679.5 23.8 %all-to-all-start.10 = ((f32[128,1,16,128]{3,2,1,0:T(8,128)}), f32[128,1,16,128]{3,2,1,0:T(8,128)}, u32[]{:S(2)}, u32[]{:S(2)}) async-start(f32[128,1,16,128]{3,2,1,0:T(8,128)} %bitcast_multiply_fusion), calls=%async_computation.10 | async-start | bytes 2097152 | tf_op jit(solution)/shard_map/all_to_all | solution.py:112
  706.0 3.7 copy-start.3
  (4 other events, 9.4 us)
